TPU v7x, 32 devices: a whole 2x2x4 slice. The times are simulated.
32 devices in a mesh: row: 8 (over z, core), col: 4 (over y, x).
Axes of the slice: x: 2, y: 2, z: 4, core: 2. Of those that a mesh axis runs over, the one named last changes fastest.
Arguments:
- gram: bfloat16 [32768, 32768], P('row', 'col'), may hold values from -1 to 5, as said below
- start_basis: bfloat16 [32768, 256], P(('row', 'col')), may hold values from -12 to 12
- slab: float32 [32768, 4096], P('row', 'col'), may hold values from -6 to 6
Outputs:
- core_scaled: float32 [32768, 256], P(('row', 'col'))
- next_unfolding: float32 [4096, 256], P(('row', 'col'))
Inputs may be any that keep to these rules, and one draw needn't show every extreme that they name: gram is symmetric: entry (i, j) equals entry (j, i).
All inputs are finite; a program needn't handle non-finite values.
Results may differ from a plain program's by a relative error of at most 0.003.
Values may be sent and summed in bfloat16 or wider, within the bound.
A program may use at most 192 MiB of HBM per device.

v0:
```python
import math
import jax
import jax.numpy as jnp
from jax import lax
from jax.sharding import PartitionSpec as P

N = 32768
NMODE = 16


def body(gram, start_basis, slab):
    col_count = lax.axis_size("col")
    highest = lax.Precision.HIGHEST
    contract_rows = (((0,), (0,)), ((), ()))
    own_rows = lax.all_gather(start_basis, "col", axis=0, tiled=True)
    first_image = lax.psum_scatter(
        lax.dot_general(gram, own_rows, contract_rows, preferred_element_type=jnp.float32),
        "row",
        scatter_dimension=0,
        tiled=True,
    ).astype(jnp.bfloat16)
    col_rows = lax.all_gather(first_image, "row", axis=0, tiled=True)
    second_image = lax.psum_scatter(
        jnp.dot(gram, col_rows, preferred_element_type=jnp.float32),
        "col",
        scatter_dimension=0,
        tiled=True,
    )
    own_gram = lax.dot_general(
        second_image,
        second_image,
        contract_rows,
        precision=highest,
        preferred_element_type=jnp.float32,
    )
    small_gram = lax.psum(own_gram, ("row", "col"))
    factor = jnp.linalg.cholesky(small_gram)
    basis_cols = jax.scipy.linalg.solve_triangular(factor, second_image.T, lower=True).T
    block_basis = lax.all_gather(basis_cols, "col", axis=0, tiled=True)
    own_proj = lax.psum_scatter(
        lax.dot_general(
            block_basis, slab, contract_rows, precision=highest, preferred_element_type=jnp.float32
        ),
        "row",
        scatter_dimension=0,
        tiled=True,
    )
    core_out = basis_cols * math.sqrt(N)
    mode_share = NMODE // col_count
    grouped = own_proj.reshape(own_proj.shape[0], mode_share, own_proj.shape[1] // mode_share)
    regrouped = lax.all_to_all(grouped, "col", split_axis=0, concat_axis=1, tiled=True)
    return (
        core_out,
        regrouped.reshape(regrouped.shape[0] * regrouped.shape[1], regrouped.shape[2]),
    )


def solution(mesh):
    in_specs = (P("row", "col"), P(("row", "col"), None), P("row", "col"))
    out_specs = (P(("row", "col"), None), P(("row", "col"), None))
    return jax.shard_map(body, mesh=mesh, in_specs=in_specs, out_specs=out_specs, check_vma=False)
```

profile of v0, /device:TPU:0, one launch (start us, length us, event | category | flops | bytes accessed | tf_op | source)
XLA Modules:
  0.0 614.0 jit_solution(10611750755675535246)
XLA Ops:
  7.9 39.8 %all-gather.4.cloned.1.call-done = bf16[4096,256]{1,0:T(8,128)(2,1)} async-done(((bf16[1024,256]{1,0:T(8,128)(2,1)}), bf16[4096,256]{1,0:T(8,128)(2,1)}) %all-gather.4.cloned.1.call-update) | async-done | bytes 2097168 | tf_op jit(solution)/shard_map/all_gather | solution.py:15
  47.8 30.0 %fusion.9 = f32[8192,256]{1,0:T(8,128)} fusion(bf16[4096,8192]{1,0:T(8,128)(2,1)} %param.3, bf16[4096,256]{1,0:T(8,128)(2,1)} %all-gather.4.cloned.1.call-done), kind=kOutput, calls=%fused_computation.32 | convolution fusion | flops 17179869184 | bytes 77594624 | tf_op jit(solution)/shard_map/dot_general | solution.py:17
  77.8 89.6 %reduce-scatter.4.cloned.1.call-done = f32[1024,256]{1,0:T(8,128)} async-done(((f32[8192,256]{1,0:T(8,128)}), f32[1024,256]{1,0:T(8,128)}) %reduce-scatter.4.cloned.1.call-update) | async-done | bytes 1048592 | tf_op jit(solution)/shard_map/reduce_scatter | solution.py:16
  167.4 2.1 convert_element_type.3
  169.6 45.4 %all-gather.6.cloned.1.call-done = bf16[8192,256]{1,0:T(8,128)(2,1)} async-done(((bf16[1024,256]{1,0:T(8,128)(2,1)}), bf16[8192,256]{1,0:T(8,128)(2,1)}) %all-gather.6.cloned.1.call-update) | async-done | bytes 4194320 | tf_op jit(solution)/shard_map/all_gather | solution.py:22
  215.0 29.2 %convolution_bitcast_fusion = f32[4096,256]{0,1:T(8,128)} fusion(bf16[8192,256]{1,0:T(8,128)(2,1)} %all-gather.6.cloned.1.call-done, bf16[4096,8192]{1,0:T(8,128)(2,1)} %param.3), kind=kOutput, calls=%fused_computation.2 | convolution fusion | flops 17179869184 | bytes 75497472 | tf_op jit(solution)/shard_map/dot_general | solution.py:24
  244.3 51.5 %reduce-scatter.6.cloned.1.call-done = f32[1024,256]{0,1:T(8,128)} async-done(((f32[4096,256]{0,1:T(8,128)}), f32[1024,256]{0,1:T(8,128)}) %reduce-scatter.6.cloned.1.call-update) | async-done | bytes 1048592 | tf_op jit(solution)/shard_map/reduce_scatter | solution.py:23
  295.8 3.4 fusion.10
  299.4 128.9 %all-reduce.3.cloned.1.call-done = f32[256,256]{0,1:T(8,128)} async-done(((f32[256,256]{0,1:T(8,128)}), f32[256,256]{0,1:T(8,128)}) %all-reduce.3.cloned.1.call-update) | async-done | bytes 262160 | tf_op jit(solution)/shard_map/psum | solution.py:36
  428.3 1.1 copy.6
  430.4 11.7 %cholesky.50 = f32[128,128]{1,0:T(8,128)S(1)} custom-call(f32[128,128]{1,0:T(8,128)S(1)} %cholesky.118), custom_call_target="Cholesky" | custom-call | tf_op jit(solution)/shard_map/jit(cholesky)/cholesky | solution.py:37
  442.1 9.8 %custom-call.15 = f32[1,128,128]{1,2,0:T(8,128)S(1)} custom-call(f32[1,128,128]{2,1,0:T(8,128)S(1)} %get-tuple-element.25), custom_call_target="InvertDiagBlocksLowerTriangular" | custom-call | tf_op jit(solution)/shard_map/jit(cholesky)/cholesky | solution.py:37
  452.4 11.7 %cholesky.105 = f32[128,128]{1,0:T(8,128)S(1)} custom-call(f32[128,128]{1,0:T(8,128)S(1)} %convolution_subtract_fusion.1), custom_call_target="Cholesky" | custom-call | tf_op jit(solution)/shard_map/jit(cholesky)/cholesky | solution.py:37
  466.4 4.3 while.1
  467.1 1.4 bitcast_dynamic-update-slice_fusion.2
  469.2 1.4 bitcast_dynamic-update-slice_fusion.2
  470.6 19.7 %custom-call.16 = f32[2,128,128]{1,2,0:T(8,128)S(1)} custom-call(f32[2,128,128]{2,1,0:T(8,128)S(1)} %get-tuple-element.9), custom_call_target="InvertDiagBlocksLowerTriangular" | custom-call | tf_op jit(solution)/shard_map/jit(_solve_triangular)/triangular_solve | solution.py:38
  493.3 51.7 %all-gather.8.cloned.1.call-done = f32[4096,256]{0,1:T(8,128)} async-done(((f32[1024,256]{0,1:T(8,128)}), f32[4096,256]{0,1:T(8,128)}) %all-gather.8.cloned.1.call-update) | async-done | bytes 4194320 | tf_op jit(solution)/shard_map/all_gather | solution.py:39
  545.1 18.3 %fusion.11 = f32[256,1024]{1,0:T(8,128)} fusion(f32[4096,256]{0,1:T(8,128)} %all-gather.8.cloned.1.call-done, f32[4096,1024]{1,0:T(8,128)} %param.5), kind=kOutput, calls=%fused_computation.34 | convolution fusion | flops 12884901888 | bytes 22020096 | tf_op jit(solution)/shard_map/dot_general | solution.py:41
  563.3 32.8 %reduce-scatter.8.cloned.1.call-done = f32[32,1024]{1,0:T(8,128)} async-done(((f32[256,1024]{1,0:T(8,128)}), f32[32,1024]{1,0:T(8,128)}) %reduce-scatter.8.cloned.1.call-update) | async-done | bytes 131088 | tf_op jit(solution)/shard_map/reduce_scatter | solution.py:40
  596.1 1.6 reshape.30
  597.7 3.7 all-to-all-start
  601.5 1.3 copy.8
  602.9 3.6 all-to-all-done
  (39 shorter events, 8.6 us)
Async XLA Ops:
  7.2 40.6 %all-gather.4.cloned.1.call-start = ((), (), s32[]{:S(2)}) async-start(), calls=%async_computation.4 | async-start | bytes 2621440 | tf_op jit(solution)/shard_map/all_gather | solution.py:15
  7.9 159.5 %reduce-scatter.4.cloned.1.call-start = ((), (), s32[]{:S(2)}) async-start(), calls=%async_computation.5 | async-start | bytes 9437184 | tf_op jit(solution)/shard_map/reduce_scatter | solution.py:16
  77.7 137.3 %all-gather.6.cloned.1.call-start = ((), (), s32[]{:S(2)}) async-start(), calls=%async_computation.6 | async-start | bytes 4718592 | tf_op jit(solution)/shard_map/all_gather | solution.py:22
  169.5 126.2 %reduce-scatter.6.cloned.1.call-start = ((), (), s32[]{:S(2)}) async-start(), calls=%async_computation.7 | async-start | bytes 5242880 | tf_op jit(solution)/shard_map/reduce_scatter | solution.py:23
  244.2 184.1 %all-reduce.3.cloned.1.call-start = ((), (), s32[]{:S(2)}) async-start(), calls=%async_computation.8 | async-start | bytes 524288 | tf_op jit(solution)/shard_map/psum | solution.py:36
  295.8 194.6 %copy-start = (f32[1024,256]{0,1:T(8,128)S(1)}, f32[1024,256]{0,1:T(8,128)}, u32[]{:S(2)}) copy-start(f32[1024,256]{0,1:T(8,128)} %reduce-scatter.6.cloned.1.call-done) | copy-start | bytes 3145732
  299.1 245.9 %all-gather.8.cloned.1.call-start = ((), (), s32[]{:S(2)}) async-start(), calls=%async_computation.9 | async-start | bytes 5242880 | tf_op jit(solution)/shard_map/all_gather | solution.py:39
  493.3 102.9 %reduce-scatter.8.cloned.1.call-start = ((), (), s32[]{:S(2)}) async-start(), calls=%async_computation.10 | async-start | bytes 1179648 | tf_op jit(solution)/shard_map/reduce_scatter | solution.py:40
  597.7 8.7 %all-to-all-start = ((f32[32,4,256]{2,1,0:T(4,128)}), f32[32,4,256]{2,1,0:T(4,128)S(1)}, u32[]{:S(2)}, u32[]{:S(2)}) async-start(f32[32,4,256]{2,1,0:T(4,128)} %reshape.30), calls=%async_computation.3 | async-start | bytes 262144 | tf_op jit(solution)/shard_map/all_to_all | solution.py:51
Sparse Core Ops, SparseCore 0:
  9.8 37.8 all-gather.3
  77.9 89.5 reduce-scatter.3
  169.6 45.3 all-gather.5
  244.3 51.3 reduce-scatter.5
  301.7 126.5 all-reduce.2
  493.4 51.6 all-gather.7
  563.5 32.6 reduce-scatter.7
where the time goes:
time: 614 us
  waiting for transfers between devices  444 us (72%)
  matrix products  83.1 us (14%)
  other arithmetic  58 us (9%)
  between operations  15.6 us (3%)
  local copies, waits for them, and re-layouts  8.87 us (1%)
    psum x1, waiting for transfers between devices, body(): small_gram = lax.psum(own_gram, ('row', 'col'))  129 us
    reduce_scatter x1, waiting for transfers between devices, body(): lax.psum_scatter(lax.dot_general(gram, own_rows, contract_rows, preferred...  89.6 us
    all_gather x1, waiting for transfers between devices, body(): block_basis = lax.all_gather(basis_cols, 'col', axis=0, tiled=True)  51.7 us
    reduce_scatter x1, waiting for transfers between devices, body(): lax.psum_scatter(jnp.dot(gram, col_rows, preferred_element_type=jnp.float...  51.5 us
    all_gather x1, waiting for transfers between devices, body(): col_rows = lax.all_gather(first_image, 'row', axis=0, tiled=True)  45.4 us
    all_gather x1, waiting for transfers between devices, body(): own_rows = lax.all_gather(start_basis, 'col', axis=0, tiled=True)  39.8 us
    another operation x6, other arithmetic, body(): factor = jnp.linalg.cholesky(small_gram)  34 us
    reduce_scatter x1, waiting for transfers between devices, body(): lax.psum_scatter(lax.dot_general(block_basis, slab, contract_rows, precis...  32.8 us
  transfers between devices with their start and end apart: 8, of which 8 were waited for; matrix products, arithmetic and copies ran while one was open for 0% of the time, Pallas kernels for 0%

commit v1 on v0

--- a/solution.py
+++ b/solution.py
@@ -6,6 +6,17 @@
 
 N = 32768
 NMODE = 16
+
+
+def pass_along(array, axis, dim):
+    size = lax.axis_size(axis)
+    right = [(i, (i + 1) % size) for i in range(size)]
+    blocks = [array]
+    for far in range(1, size):
+        blocks = [lax.ppermute(blocks[0], axis, right), *blocks]
+    whole = jnp.concatenate(blocks, axis=dim)
+    turn = (lax.axis_index(axis) + 1) * blocks[-1].shape[dim]
+    return jnp.roll(whole, turn, axis=dim)
 
 
 def body(gram, start_basis, slab):
@@ -36,7 +47,7 @@
     small_gram = lax.psum(own_gram, ("row", "col"))
     factor = jnp.linalg.cholesky(small_gram)
     basis_cols = jax.scipy.linalg.solve_triangular(factor, second_image.T, lower=True).T
-    block_basis = lax.all_gather(basis_cols, "col", axis=0, tiled=True)
+    block_basis = pass_along(basis_cols, "col", 0)
     own_proj = lax.psum_scatter(
         lax.dot_general(
             block_basis, slab, contract_rows, precision=highest, preferred_element_type=jnp.float32

time: 614 us -> 636 us (1.036)
  waiting for transfers between devices: 444 us -> 460 us
    ppermute x0 -> x3, waiting for transfers between devices: none -> 70.5 us  [pass_along(): blocks = [lax.ppermute(blocks[0], axis, right), *blocks]]
    all_gather x1 -> x0, waiting for transfers between devices: 51.7 us -> none  [body(): block_basis = lax.all_gather(basis_cols, 'col', axis=0, tiled=True)]
  transfers between devices with their start and end apart: 8 -> 10, of which waited for: 8 -> 10; matrix products, arithmetic and copies ran while one was open for 0% -> 0% of each run, Pallas kernels for 0% -> 0%
where the time goes in v1:
time: 636 us
  waiting for transfers between devices  460 us (72%)
  matrix products  84.2 us (13%)
  other arithmetic  57.3 us (9%)
  between operations  15.6 us (2%)
  local copies, waits for them, and re-layouts  11.9 us (2%)
    psum x1, waiting for transfers between devices, body(): small_gram = lax.psum(own_gram, ('row', 'col'))  129 us
    reduce_scatter x1, waiting for transfers between devices, body(): lax.psum_scatter(lax.dot_general(gram, own_rows, contract_rows, preferred...  89.6 us
    ppermute x3, waiting for transfers between devices, pass_along(): blocks = [lax.ppermute(blocks[0], axis, right), *blocks]  70.5 us
    reduce_scatter x1, waiting for transfers between devices, body(): lax.psum_scatter(jnp.dot(gram, col_rows, preferred_element_type=jnp.float...  51.5 us
    all_gather x1, waiting for transfers between devices, body(): col_rows = lax.all_gather(first_image, 'row', axis=0, tiled=True)  45.4 us
    all_gather x1, waiting for transfers between devices, body(): own_rows = lax.all_gather(start_basis, 'col', axis=0, tiled=True)  39.8 us
    another operation x6, other arithmetic, body(): factor = jnp.linalg.cholesky(small_gram)  34 us
    reduce_scatter x1, waiting for transfers between devices, body(): lax.psum_scatter(lax.dot_general(block_basis, slab, contract_rows, precis...  30 us
  transfers between devices with their start and end apart: 10, of which 10 were waited for; matrix products, arithmetic and copies ran while one was open for 0% of the time, Pallas kernels for 0%

profile of v1, /device:TPU:0, one launch (start us, length us, event | category | flops | bytes accessed | tf_op | source)
XLA Modules:
  0.0 635.6 jit_solution(4162626087289670230)
XLA Ops:
  7.9 39.8 %all-gather.3.cloned.1.call-done = bf16[4096,256]{1,0:T(8,128)(2,1)} async-done(((bf16[1024,256]{1,0:T(8,128)(2,1)}), bf16[4096,256]{1,0:T(8,128)(2,1)}) %all-gather.3.cloned.1.call-update) | async-done | bytes 2097168 | tf_op jit(solution)/shard_map/all_gather | solution.py:26
  47.8 30.0 %fusion.12 = f32[8192,256]{1,0:T(8,128)} fusion(bf16[4096,8192]{1,0:T(8,128)(2,1)} %param.3, bf16[4096,256]{1,0:T(8,128)(2,1)} %all-gather.3.cloned.1.call-done), kind=kOutput, calls=%fused_computation.43 | convolution fusion | flops 17179869184 | bytes 77594624 | tf_op jit(solution)/shard_map/dot_general | solution.py:28
  77.8 89.6 %reduce-scatter.4.cloned.1.call-done = f32[1024,256]{1,0:T(8,128)} async-done(((f32[8192,256]{1,0:T(8,128)}), f32[1024,256]{1,0:T(8,128)}) %reduce-scatter.4.cloned.1.call-update) | async-done | bytes 1048592 | tf_op jit(solution)/shard_map/reduce_scatter | solution.py:27
  167.4 2.1 convert_element_type.3
  169.6 45.4 %all-gather.5.cloned.1.call-done = bf16[8192,256]{1,0:T(8,128)(2,1)} async-done(((bf16[1024,256]{1,0:T(8,128)(2,1)}), bf16[8192,256]{1,0:T(8,128)(2,1)}) %all-gather.5.cloned.1.call-update) | async-done | bytes 4194320 | tf_op jit(solution)/shard_map/all_gather | solution.py:33
  215.0 29.2 %convolution_bitcast_fusion = f32[4096,256]{0,1:T(8,128)} fusion(bf16[8192,256]{1,0:T(8,128)(2,1)} %all-gather.5.cloned.1.call-done, bf16[4096,8192]{1,0:T(8,128)(2,1)} %param.3), kind=kOutput, calls=%fused_computation.2 | convolution fusion | flops 17179869184 | bytes 75497472 | tf_op jit(solution)/shard_map/dot_general | solution.py:35
  244.3 51.5 %reduce-scatter.6.cloned.1.call-done = f32[1024,256]{0,1:T(8,128)} async-done(((f32[4096,256]{0,1:T(8,128)}), f32[1024,256]{0,1:T(8,128)}) %reduce-scatter.6.cloned.1.call-update) | async-done | bytes 1048592 | tf_op jit(solution)/shard_map/reduce_scatter | solution.py:34
  295.8 3.3 fusion.13
  299.3 129.0 %all-reduce.3.cloned.1.call-done = f32[256,256]{0,1:T(8,128)} async-done(((f32[256,256]{0,1:T(8,128)}), f32[256,256]{0,1:T(8,128)}) %all-reduce.3.cloned.1.call-update) | async-done | bytes 262160 | tf_op jit(solution)/shard_map/psum | solution.py:47
  430.4 11.7 %cholesky.50 = f32[128,128]{1,0:T(8,128)S(1)} custom-call(f32[128,128]{1,0:T(8,128)S(1)} %cholesky.118), custom_call_target="Cholesky" | custom-call | tf_op jit(solution)/shard_map/jit(cholesky)/cholesky | solution.py:48
  442.1 9.8 %custom-call.15 = f32[1,128,128]{1,2,0:T(8,128)S(1)} custom-call(f32[1,128,128]{2,1,0:T(8,128)S(1)} %get-tuple-element.27), custom_call_target="InvertDiagBlocksLowerTriangular" | custom-call | tf_op jit(solution)/shard_map/jit(cholesky)/cholesky | solution.py:48
  452.4 11.7 %cholesky.105 = f32[128,128]{1,0:T(8,128)S(1)} custom-call(f32[128,128]{1,0:T(8,128)S(1)} %convolution_subtract_fusion.1), custom_call_target="Cholesky" | custom-call | tf_op jit(solution)/shard_map/jit(cholesky)/cholesky | solution.py:48
  466.4 4.3 while.1
  470.6 19.7 %custom-call.16 = f32[2,128,128]{1,2,0:T(8,128)S(1)} custom-call(f32[2,128,128]{2,1,0:T(8,128)S(1)} %get-tuple-element.9), custom_call_target="InvertDiagBlocksLowerTriangular" | custom-call | tf_op jit(solution)/shard_map/jit(_solve_triangular)/triangular_solve | solution.py:49
  490.3 1.7 fusion.2
  492.0 1.6 convolution_subtract_fusion
  495.9 23.5 %collective-permute-done = f32[1024,256]{0,1:T(8,128)S(1)} collective-permute-done((f32[1024,256]{0,1:T(8,128)S(1)}, f32[1024,256]{0,1:T(8,128)S(1)}, u32[]{:S(2)}, u32[]{:S(2)}) %collective-permute-start) | collective-permute-done | bytes 1048608 | tf_op jit(solution)/shard_map/ppermute | solution.py:16
  520.0 23.6 %collective-permute-done.1 = f32[1024,256]{0,1:T(8,128)S(1)} collective-permute-done((f32[1024,256]{0,1:T(8,128)S(1)}, f32[1024,256]{0,1:T(8,128)S(1)}, u32[]{:S(2)}, u32[]{:S(2)}) %collective-permute-start.1) | collective-permute-done | bytes 1048608 | tf_op jit(solution)/shard_map/ppermute | solution.py:16
  543.6 23.4 %collective-permute-done.2 = f32[1024,256]{0,1:T(8,128)} collective-permute-done((f32[1024,256]{0,1:T(8,128)S(1)}, f32[1024,256]{0,1:T(8,128)}, u32[]{:S(2)}, u32[]{:S(2)}) %collective-permute-start.2) | collective-permute-done | bytes 1048608 | tf_op jit(solution)/shard_map/ppermute | solution.py:16
  570.4 17.4 %fusion = f32[256,1024]{1,0:T(8,128)} fusion(f32[4096,1024]{1,0:T(8,128)} %param.5, f32[8192,256]{0,1:T(8,128)S(1)} %get-tuple-element.22, s32[]{:T(128)S(6)} %select_n.19), kind=kOutput, calls=%fused_computation.3 | convolution fusion | flops 12884901888 | bytes 22020100 | tf_op jit(solution)/shard_map/dot_general | solution.py:52
  587.8 30.0 %reduce-scatter.8.cloned.1.call-done = f32[32,1024]{1,0:T(8,128)} async-done(((f32[256,1024]{1,0:T(8,128)}), f32[32,1024]{1,0:T(8,128)}) %reduce-scatter.8.cloned.1.call-update) | async-done | bytes 131088 | tf_op jit(solution)/shard_map/reduce_scatter | solution.py:51
  617.8 1.6 reshape.30
  619.5 3.5 all-to-all-start
  624.3 3.7 all-to-all-done
  (47 shorter events, 16.9 us)
Async XLA Ops:
  7.2 40.6 %all-gather.3.cloned.1.call-start = ((), (), s32[]{:S(2)}) async-start(), calls=%async_computation.4 | async-start | bytes 2621440 | tf_op jit(solution)/shard_map/all_gather | solution.py:26
  7.9 159.5 %reduce-scatter.4.cloned.1.call-start = ((), (), s32[]{:S(2)}) async-start(), calls=%async_computation.5 | async-start | bytes 9437184 | tf_op jit(solution)/shard_map/reduce_scatter | solution.py:27
  77.7 137.3 %all-gather.5.cloned.1.call-start = ((), (), s32[]{:S(2)}) async-start(), calls=%async_computation.6 | async-start | bytes 4718592 | tf_op jit(solution)/shard_map/all_gather | solution.py:33
  169.5 126.2 %reduce-scatter.6.cloned.1.call-start = ((), (), s32[]{:S(2)}) async-start(), calls=%async_computation.7 | async-start | bytes 5242880 | tf_op jit(solution)/shard_map/reduce_scatter | solution.py:34
  244.2 184.1 %all-reduce.3.cloned.1.call-start = ((), (), s32[]{:S(2)}) async-start(), calls=%async_computation.8 | async-start | bytes 524288 | tf_op jit(solution)/shard_map/psum | solution.py:47
  299.1 318.8 %reduce-scatter.8.cloned.1.call-start = ((), (), s32[]{:S(2)}) async-start(), calls=%async_computation.9 | async-start | bytes 1179648 | tf_op jit(solution)/shard_map/reduce_scatter | solution.py:51
  494.4 25.1 %collective-permute-start = (f32[1024,256]{0,1:T(8,128)S(1)}, f32[1024,256]{0,1:T(8,128)S(1)}, u32[]{:S(2)}, u32[]{:S(2)}) collective-permute-start(f32[1024,256]{0,1:T(8,128)S(1)} %maximum_bitcast_fusion), channel_id=1, source_target_pairs={{0,1},{1,2},{2,3},{3,0},{4,5},{5,6},{6,7},{7,4},{8,9},{9,10},{10,1... | collective-permute-start | bytes 3145736 | tf_op jit(solution)/shard_map/ppermute | solution.py:16
  519.4 24.1 %collective-permute-start.1 = (f32[1024,256]{0,1:T(8,128)S(1)}, f32[1024,256]{0,1:T(8,128)S(1)}, u32[]{:S(2)}, u32[]{:S(2)}) collective-permute-start(f32[1024,256]{0,1:T(8,128)S(1)} %collective-permute-done), channel_id=1, source_target_pairs={{0,1},{1,2},{2,3},{3,0},{4,5},{5,6},{6,7},{7,4},{8,9},{9,10},{10,1... | collective-permute-start | bytes 3145736 | tf_op jit(solution)/shard_map/ppermute | solution.py:16
  543.6 23.4 %collective-permute-start.2 = (f32[1024,256]{0,1:T(8,128)S(1)}, f32[1024,256]{0,1:T(8,128)}, u32[]{:S(2)}, u32[]{:S(2)}) collective-permute-start(f32[1024,256]{0,1:T(8,128)S(1)} %collective-permute-done.1), channel_id=1, source_target_pairs={{0,1},{1,2},{2,3},{3,0},{4,5},{5,6},{6,7},{7,4},{8,9},{9,10},{10,1... | collective-permute-start | bytes 3145736 | tf_op jit(solution)/shard_map/ppermute | solution.py:16
  619.5 8.6 %all-to-all-start = ((f32[32,4,256]{2,1,0:T(4,128)}), f32[32,4,256]{2,1,0:T(4,128)S(1)}, u32[]{:S(2)}, u32[]{:S(2)}) async-start(f32[32,4,256]{2,1,0:T(4,128)} %reshape.30), calls=%async_computation.3 | async-start | bytes 262144 | tf_op jit(solution)/shard_map/all_to_all | solution.py:62
Sparse Core Ops, SparseCore 0:
  9.8 37.8 all-gather.2
  77.9 89.5 reduce-scatter.3
  169.6 45.3 all-gather.4
  244.3 51.3 reduce-scatter.5
  301.7 126.5 all-reduce.2
  587.9 29.8 reduce-scatter.7
